TPU v7x, 256 devices: a whole 4x4x8 slice. The times are simulated.
256 devices in a mesh: dp: 32 (over x, y, core), mp: 8 (over z).
Axes of the slice: x: 4, y: 4, z: 8, core: 2. Of those that a mesh axis runs over, the one named last changes fastest.
Arguments:
- queries: bfloat16 [4096, 64, 128], P('dp', 'mp'), may hold values from -6 to 6
- key_cache: bfloat16 [4096, 8, 128, 128], P('dp', 'mp'), may hold values from -6 to 6
- value_cache: bfloat16 [4096, 8, 128, 128], P('dp', 'mp'), may hold values from -6 to 6
- key_new: bfloat16 [4096, 8, 128], P('dp', 'mp'), may hold values from -6 to 6
- value_new: bfloat16 [4096, 8, 128], P('dp', 'mp'), may hold values from -6 to 6
- lengths: int32 [4096], P('dp'), may hold values from 1 to 128, as said below
- occupied: int32 [4096], P('dp'), may hold values 0 or 1
- slot_request: int32 [4096], P('dp'), may hold values from 0 to 4095, as said below
- request_adapter: int32 [4096], replicated, may hold values from 0 to 63, as said below
- out_weight: bfloat16 [8192, 4096], P('mp'), may hold values from -0.375 to 0.375
- shrink_weight: bfloat16 [64, 8192, 64], P('dp', 'mp'), may hold values from -0.375 to 0.375
- expand_weight: bfloat16 [64, 64, 4096], P('dp', None, 'mp'), may hold values from -0.75 to 0.75
Outputs:
- mixed: bfloat16 [4096, 4096], P('dp', 'mp')
Inputs may be any that keep to these rules, and one draw needn't show every extreme that they name: `slot_request`: A permutation: each request stands in exactly one slot. `request_adapter`: adapter n is owned by dp index n // 2. Among the slots of one dp index, at most 8 hold requests whose adapters one dp index owns; in every draw some dp index owns the adapters of exactly 8 slots of every dp index. `lengths`: each dp index has a slot of length 128.
All inputs are finite; a program needn't handle non-finite values. No bound on the sum of `occupied` on one device may be relied on, other than what follows from the above.
Results may differ from a plain program's by a relative error of at most 0.011.
Values may be sent and summed in bfloat16 or wider, within the bound.
A program may use at most 64 MiB of HBM per device.

v0:
```python
import math
import jax
import jax.numpy as jnp
from jax import lax
from jax.sharding import PartitionSpec as P


def attend(queries, key_cache, value_cache, key_new, value_new, lengths):
    rows, heads, width = queries.shape
    kv_local = key_cache.shape[1]
    group = heads // kv_local
    inverse = 1.0 / math.sqrt(width)
    grouped = queries.reshape(rows, kv_local, group, width)
    cached = (
        jnp.einsum("bgjd,bgtd->bgjt", grouped, key_cache, preferred_element_type=jnp.float32)
        * inverse
    )
    fresh = (
        jnp.einsum("bgjd,bgd->bgj", grouped, key_new, preferred_element_type=jnp.float32) * inverse
    )
    valid = jnp.arange(key_cache.shape[2])[None, :] < lengths[:, None]
    cached = jnp.where(valid[:, None, None, :], cached, -jnp.inf)
    top = jnp.maximum(jnp.max(cached, axis=-1), fresh)
    cached_exp = jnp.exp(cached - top[..., None])
    fresh_exp = jnp.exp(fresh - top)
    total = jnp.sum(cached_exp, axis=-1) + fresh_exp
    cached_w = (cached_exp / total[..., None]).astype(jnp.bfloat16)
    fresh_w = (fresh_exp / total).astype(jnp.bfloat16)
    summed = jnp.einsum(
        "bgjt,bgtd->bgjd", cached_w, value_cache, preferred_element_type=jnp.float32
    )
    summed = (
        summed
        + fresh_w.astype(jnp.float32)[..., None] * value_new.astype(jnp.float32)[:, :, None, :]
    )
    return summed.reshape(rows, heads * width).astype(jnp.bfloat16)


def body(
    queries,
    key_cache,
    value_cache,
    key_new,
    value_new,
    lengths,
    occupied,
    slot_request,
    request_adapter,
    out_weight,
    shrink_weight,
    expand_weight,
):
    rows = queries.shape[0]
    attended = attend(queries, key_cache, value_cache, key_new, value_new, lengths)
    owners_count = lax.axis_size("dp")
    adapters_here = shrink_weight.shape[0]
    rank_width = shrink_weight.shape[2]
    out_local = expand_weight.shape[2]
    capacity = 2 * rows // owners_count
    matches = (
        slot_request[:, None] == jnp.arange(request_adapter.shape[0], dtype=jnp.int32)[None, :]
    )
    slot_adapter = jnp.sum(jnp.where(matches, request_adapter[None, :], 0), axis=1)
    owner = slot_adapter // adapters_here
    local_ids = slot_adapter % adapters_here
    owner_onehot = (owner[:, None] == jnp.arange(owners_count, dtype=jnp.int32)[None, :]).astype(
        jnp.int32
    )
    earlier = jnp.cumsum(owner_onehot, axis=0) - owner_onehot
    position = jnp.sum(earlier * owner_onehot, axis=1)
    slot_code = owner * capacity + position
    dispatch = jnp.arange(owners_count * capacity, dtype=jnp.int32)[:, None] == slot_code[None, :]
    send_rows = jnp.dot(
        dispatch.astype(jnp.bfloat16), attended, preferred_element_type=jnp.float32
    ).astype(jnp.bfloat16)
    send_rows = send_rows.reshape(owners_count, capacity, attended.shape[1])
    send_ids = jnp.sum(jnp.where(dispatch, (local_ids + 1)[None, :], 0), axis=1).reshape(
        owners_count, capacity
    )
    combine = (
        slot_code[:, None] == jnp.arange(owners_count * capacity, dtype=jnp.int32)[None, :]
    ).astype(jnp.bfloat16)
    partial_value = jnp.dot(attended, out_weight, preferred_element_type=jnp.float32)
    full = lax.psum(partial_value, "mp")
    base = lax.dynamic_slice_in_dim(full, lax.axis_index("mp") * out_local, out_local, 1)
    got_rows = lax.all_to_all(send_rows, "dp", split_axis=0, concat_axis=0, tiled=True)
    got_ids = lax.all_to_all(send_ids, "dp", split_axis=0, concat_axis=0, tiled=True)
    flat = got_rows.reshape(owners_count * capacity, got_rows.shape[2])
    wanted = got_ids.reshape(owners_count * capacity) - 1
    partial_value = jnp.einsum(
        "md,adr->mar", flat, shrink_weight, preferred_element_type=jnp.float32
    )
    which = jnp.arange(adapters_here, dtype=jnp.int32)[None, :] == wanted[:, None]
    partial_value = jnp.where(which[:, :, None], partial_value, 0.0)
    summed = lax.psum(
        partial_value.reshape(owners_count * capacity, adapters_here * rank_width), "mp"
    )
    low = summed.astype(jnp.bfloat16).reshape(owners_count * capacity, adapters_here, rank_width)
    delta = 0.5 * jnp.einsum("mar,are->me", low, expand_weight, preferred_element_type=jnp.float32)
    delta = delta.astype(jnp.bfloat16).reshape(owners_count, capacity, out_local)
    back = lax.all_to_all(delta, "dp", split_axis=0, concat_axis=0, tiled=True)
    correction = jnp.dot(
        combine,
        back.reshape(owners_count * capacity, out_local),
        preferred_element_type=jnp.float32,
    )
    return (occupied.astype(jnp.float32)[:, None] * (base + correction)).astype(jnp.bfloat16)


def solution(mesh):
    placed = (
        P("dp", "mp", None),
        P("dp", "mp", None, None),
        P("dp", "mp", None, None),
        P("dp", "mp", None),
        P("dp", "mp", None),
        P("dp"),
        P("dp"),
        P("dp"),
        P(),
        P("mp", None),
        P("dp", "mp", None),
        P("dp", None, "mp"),
    )
    return jax.shard_map(body, mesh=mesh, in_specs=placed, out_specs=P("dp", "mp"), check_vma=False)
```

profile of v0, /device:TPU:22, one launch (start us, length us, event | category | flops | bytes accessed | tf_op | source)
XLA Modules:
  0.0 117.1 jit_solution(17132844115245272164)
XLA Ops:
  6.5 0.0 copy-start
  6.5 0.0 copy-start.1
  6.5 0.0 copy-start.6
  6.5 0.0 copy-start.3
  6.5 0.0 all-reduce.3.cloned.1.call-start
  6.6 0.8 iota_compare_fusion.6
  7.4 4.6 %fusion.42 = (f32[128,8]{1,0:T(8,128)S(1)}, f32[128,8,128]{2,1,0:T(8,128)S(1)}) fusion(bf16[128,8,128]{2,1,0:T(8,128)(2,1)} %param.12, bf16[128,1,128,128]{3,2,1,0:T(8,128)(2,1)} %param.13, pred[128,128]{1,0:T(8,128)(4,1)S(1)} %iota_compare_fusion.6), kind=kOutput, calls=%fused_computation.60 | convolution fusion | flops 33946624 | bytes 5001216 | tf_op jit(solution)/shard_map/bgjd,bgtd->bgjt/dot_general | solution.py:15
  12.0 0.1 copy.19
  12.1 0.0 copy-done.1
  12.1 0.0 copy-done.6
  12.1 0.3 fusion.36
  12.4 0.1 copy.20
  12.6 0.4 fusion.24
  13.0 0.1 copy.22
  13.1 0.1 copy.23
  13.2 0.0 copy-done.3
  13.3 3.5 %fusion.16 = bf16[128,8,128]{2,1,0:T(8,128)(2,1)S(1)} fusion(bf16[128,1,128,128]{3,2,1,0:T(8,128)(2,1)} %param.14, f32[128,8,128]{2,1,0:T(8,128)S(1)} %get-tuple-element.10, f32[128,128]{1,0:T(8,128)S(1)} %bitcast_convert_fusion, f32[128,8]{1,0:T(8,128)S(1)} %copy.23, f32[128,8]{1,0:T(8,128)S(1)} %copy.22, f32[128,8]{1,0:T(8,128)S(1)} %copy.20), kind=kOutput, calls=%fused_computation.14 | convolution fusion | flops 34340864 | bytes 5058560 | tf_op jit(solution)/shard_map/bgjt,bgtd->bgjd/dot_general | solution.py:29
  16.7 0.0 copy-start.4
  16.7 0.0 copy-start.5
  16.7 6.0 %fusion.26 = f32[128,4096]{1,0:T(8,128)} fusion(bf16[1024,4096]{1,0:T(8,128)(2,1)} %param.21, bf16[16,8,8,128]{3,2,1,0:T(8,128)(2,1)S(1)} %bitcast.75), kind=kOutput, calls=%fused_computation.25 | convolution fusion | flops 1073741824 | bytes 10747904 | tf_op jit(solution)/shard_map/dot_general | solution.py:83
  22.7 0.0 copy-start.2
  22.7 0.0 copy-start.7
  22.7 0.0 all-reduce.3.cloned.1.call-update
  22.7 0.0 copy-done.4
  22.8 0.0 copy-done.5
  22.8 0.4 select_reduce_fusion
  23.2 0.1 fusion.35
  23.3 0.2 reduce_window_sum.11
  23.5 0.2 select_reduce_fusion.2
  23.7 0.1 select_reduce_fusion.1
  23.8 0.7 all_to_all.12
  24.5 7.4 %all-to-all-start = ((s32[32,1,8]{2,1,0:T(1,128)}), s32[32,1,8]{2,1,0:T(1,128)S(1)}, u32[]{:S(2)}, u32[]{:S(2)}) async-start(s32[32,1,8]{2,1,0:T(1,128)} %bitcast.6), calls=%async_computation | async-start | bytes 32768 | tf_op jit(solution)/shard_map/all_to_all | solution.py:87
  31.9 1.1 fusion.4
  33.0 2.5 %all-to-all-done = s32[32,1,8]{2,1,0:T(1,128)S(1)} async-done(((s32[32,1,8]{2,1,0:T(1,128)}), s32[32,1,8]{2,1,0:T(1,128)S(1)}, u32[]{:S(2)}, u32[]{:S(2)}) %all-to-all-start) | async-done | bytes 1056 | tf_op jit(solution)/shard_map/all_to_all | solution.py:87
  35.4 7.6 %all-to-all-start.1 = ((bf16[32,8,1024]{2,1,0:T(8,128)(2,1)}), bf16[32,8,1024]{2,1,0:T(8,128)(2,1)S(1)}, u32[]{:S(2)}, u32[]{:S(2)}) async-start(bf16[32,8,1024]{2,1,0:T(8,128)(2,1)} %fusion.4), calls=%async_computation.1 | async-start | bytes 1048576 | tf_op jit(solution)/shard_map/all_to_all | solution.py:86
  43.1 0.1 sub.34
  43.2 7.9 %all-to-all-done.1 = bf16[32,8,1024]{2,1,0:T(8,128)(2,1)S(1)} async-done(((bf16[32,8,1024]{2,1,0:T(8,128)(2,1)}), bf16[32,8,1024]{2,1,0:T(8,128)(2,1)S(1)}, u32[]{:S(2)}, u32[]{:S(2)}) %all-to-all-start.1) | async-done | bytes 524320 | tf_op jit(solution)/shard_map/all_to_all | solution.py:86
  51.1 0.0 copy-done
  51.1 0.3 fusion.22
  51.5 34.2 %all-reduce.4 = bf16[256,128]{0,1:T(8,128)(2,1)S(1)} all-reduce(f32[256,128]{0,1:T(8,128)S(1)} %bitcast.78), channel_id=1, replica_groups=mesh['dp'=32,'mp'=8] {'mp'}, use_global_device_ids=true, to_apply=%region_7.8 | all-reduce | flops 32768 | bytes 196608 | tf_op jit(solution)/shard_map/psum | solution.py:95
  85.7 0.0 copy-done.2
  85.7 0.9 fusion.19
  86.6 7.1 %all-to-all-start.2 = ((bf16[32,8,512]{2,1,0:T(8,128)(2,1)}), bf16[32,8,512]{2,1,0:T(8,128)(2,1)S(1)}, u32[]{:S(2)}, u32[]{:S(2)}) async-start(bf16[32,8,512]{2,1,0:T(8,128)(2,1)} %fusion.19), calls=%async_computation.2 | async-start | bytes 524288 | tf_op jit(solution)/shard_map/all_to_all | solution.py:101
  93.8 0.0 copy-done.7
  93.8 5.3 %all-to-all-done.2 = bf16[32,8,512]{2,1,0:T(8,128)(2,1)S(1)} async-done(((bf16[32,8,512]{2,1,0:T(8,128)(2,1)}), bf16[32,8,512]{2,1,0:T(8,128)(2,1)S(1)}, u32[]{:S(2)}, u32[]{:S(2)}) %all-to-all-start.2) | async-done | bytes 262176 | tf_op jit(solution)/shard_map/all_to_all | solution.py:101
  99.1 9.4 %all-reduce.3.cloned.1.call-done = f32[128,4096]{1,0:T(8,128)} async-done(((f32[128,4096]{1,0:T(8,128)}), f32[128,4096]{1,0:T(8,128)}) %all-reduce.3.cloned.1.call-update) | async-done | bytes 2097168 | tf_op jit(solution)/shard_map/psum | solution.py:84
  108.5 1.8 %fusion.21 = bf16[128,512]{1,0:T(8,128)(2,1)} fusion(bf16[32,8,512]{2,1,0:T(8,128)(2,1)S(1)} %all-to-all-done.2, f32[128,4096]{1,0:T(8,128)} %all-reduce.3.cloned.1.call-done, s32[]{:T(128)S(6)} %select_n.48, f32[128]{0:T(128)S(1)} %convert_element_type.39, s32[128]{0:T(128)S(1)} %multiply_add_fusion), kind=kOutput, calls=%fused_computation.18 | convolution fusion | flops 33783808 | bytes 656388 | tf_op jit(solution)/shard_map/dot_general | solution.py:102
  (11 shorter events, 0.2 us)
Async XLA Ops:
  6.5 44.6 %copy-start = (bf16[2,1024,64]{1,2,0:T(8,128)(2,1)S(1)}, bf16[2,1024,64]{1,2,0:T(8,128)(2,1)}, u32[]{:S(2)}) copy-start(bf16[2,1024,64]{1,2,0:T(8,128)(2,1)} %param.22) | copy-start | bytes 786436
  6.5 5.5 %copy-start.1 = (bf16[128,8,128]{2,1,0:T(8,128)(2,1)S(1)}, bf16[128,8,128]{2,1,0:T(8,128)(2,1)}, u32[]{:S(2)}) copy-start(bf16[128,8,128]{2,1,0:T(8,128)(2,1)} %param.12) | copy-start | bytes 786436
  6.5 5.5 %copy-start.6 = (bf16[128,1,128]{2,0,1:T(8,128)(2,1)S(1)}, bf16[128,1,128]{2,0,1:T(8,128)(2,1)}, u32[]{:S(2)}) copy-start(bf16[128,1,128]{2,0,1:T(8,128)(2,1)} %param.15) | copy-start | bytes 98308
  6.5 6.7 %copy-start.3 = (bf16[128,1,128]{2,0,1:T(8,128)(2,1)S(1)}, bf16[128,1,128]{2,0,1:T(8,128)(2,1)}, u32[]{:S(2)}) copy-start(bf16[128,1,128]{2,0,1:T(8,128)(2,1)} %param.16) | copy-start | bytes 98308
  6.5 101.9 %all-reduce.3.cloned.1.call-start = ((), (), s32[]{:S(2)}) async-start(), calls=%async_computation.3 | async-start | bytes 4194304 | tf_op jit(solution)/shard_map/psum | solution.py:84
  16.7 6.0 %copy-start.4 = (s32[4096]{0:T(1024)S(1)}, s32[4096]{0:T(1024)}, u32[]{:S(2)}) copy-start(s32[4096]{0:T(1024)} %param.20) | copy-start | bytes 49156
  16.7 6.0 %copy-start.5 = (s32[128]{0:T(128)S(1)}, s32[128]{0:T(128)}, u32[]{:S(2)}) copy-start(s32[128]{0:T(128)} %param.19) | copy-start | bytes 1540
  22.7 63.0 %copy-start.2 = (bf16[2,64,512]{2,1,0:T(8,128)(2,1)S(1)}, bf16[2,64,512]{2,1,0:T(8,128)(2,1)}, u32[]{:S(2)}) copy-start(bf16[2,64,512]{2,1,0:T(8,128)(2,1)} %param.23) | copy-start | bytes 393220
  22.7 71.1 %copy-start.7 = (s32[128]{0:T(128)S(1)}, s32[128]{0:T(128)}, u32[]{:S(2)}) copy-start(s32[128]{0:T(128)} %param.18) | copy-start | bytes 1540
  24.5 11.0 %all-to-all-start = ((s32[32,1,8]{2,1,0:T(1,128)}), s32[32,1,8]{2,1,0:T(1,128)S(1)}, u32[]{:S(2)}, u32[]{:S(2)}) async-start(s32[32,1,8]{2,1,0:T(1,128)} %bitcast.6), calls=%async_computation | async-start | bytes 32768 | tf_op jit(solution)/shard_map/all_to_all | solution.py:87
  35.4 15.7 %all-to-all-start.1 = ((bf16[32,8,1024]{2,1,0:T(8,128)(2,1)}), bf16[32,8,1024]{2,1,0:T(8,128)(2,1)S(1)}, u32[]{:S(2)}, u32[]{:S(2)}) async-start(bf16[32,8,1024]{2,1,0:T(8,128)(2,1)} %fusion.4), calls=%async_computation.1 | async-start | bytes 1048576 | tf_op jit(solution)/shard_map/all_to_all | solution.py:86
  86.6 12.4 %all-to-all-start.2 = ((bf16[32,8,512]{2,1,0:T(8,128)(2,1)}), bf16[32,8,512]{2,1,0:T(8,128)(2,1)S(1)}, u32[]{:S(2)}, u32[]{:S(2)}) async-start(bf16[32,8,512]{2,1,0:T(8,128)(2,1)} %fusion.19), calls=%async_computation.2 | async-start | bytes 524288 | tf_op jit(solution)/shard_map/all_to_all | solution.py:101
Sparse Core Ops, SparseCore 0:
  22.9 85.5 all-reduce.2
where the time goes:
time: 118 us; the launch traced here: 117 us
  blocking collectives  34.2 us (29%)
  waiting for transfers between devices  25.1 us (21%)
  starting transfers between devices  22.2 us (19%)
  matrix products  18.5 us (16%)
  between operations  13.6 us (12%)
  other arithmetic  2.26 us (2%)
  local copies, waits for them, and re-layouts  1.31 us (1%)
    psum x1, blocking collectives, body(): lax.psum(partial_value.reshape(owners_count * capacity, adapters_here * r...  34.2 us
    psum x1, waiting for transfers between devices, body(): full = lax.psum(partial_value, 'mp')  9.39 us
    all_to_all x1, waiting for transfers between devices, body(): lax.all_to_all(send_rows, 'dp', split_axis=0, concat_axis=0, tiled=True)  7.91 us
    all_to_all x1, starting transfers between devices, body(): lax.all_to_all(send_rows, 'dp', split_axis=0, concat_axis=0, tiled=True)  7.63 us
    all_to_all x1, starting transfers between devices, body(): lax.all_to_all(send_ids, 'dp', split_axis=0, concat_axis=0, tiled=True)  7.41 us
    all_to_all x1, starting transfers between devices, body(): back = lax.all_to_all(delta, 'dp', split_axis=0, concat_axis=0, tiled=True)  7.14 us
    dot_general x1, matrix products, body(): jnp.dot(attended, out_weight, preferred_element_type=jnp.float32)  5.97 us
    all_to_all x1, waiting for transfers between devices, body(): back = lax.all_to_all(delta, 'dp', split_axis=0, concat_axis=0, tiled=True)  5.27 us
  transfers between devices with their start and end apart: 4, of which 4 were waited for; matrix products, arithmetic and copies ran while one was open for 3% of the time, Pallas kernels for 0%

commit v1 on v0

--- a/solution.py
+++ b/solution.py
@@ -81,7 +81,16 @@
         slot_code[:, None] == jnp.arange(owners_count * capacity, dtype=jnp.int32)[None, :]
     ).astype(jnp.bfloat16)
     partial_value = jnp.dot(attended, out_weight, preferred_element_type=jnp.float32)
-    full = lax.psum(partial_value, "mp")
+
+    def close_the_keys(buf, row_axis):
+        ndev = lax.axis_size(row_axis)
+        all_rows = buf
+        for q in [[(no, no ^ rr) for no in range(ndev)] for rr in (1, 2, 4, 8, 16) if rr < ndev]:
+            b_now = lax.ppermute(all_rows, row_axis, perm=q)
+            all_rows = all_rows + b_now
+        return all_rows
+
+    full = close_the_keys(partial_value, "mp")
     base = lax.dynamic_slice_in_dim(full, lax.axis_index("mp") * out_local, out_local, 1)
     got_rows = lax.all_to_all(send_rows, "dp", split_axis=0, concat_axis=0, tiled=True)
     got_ids = lax.all_to_all(send_ids, "dp", split_axis=0, concat_axis=0, tiled=True)

time: 118 us -> 298 us (2.53); the launches traced: 117 us -> 293 us
  waiting for transfers between devices: 25.1 us -> 151 us
  blocking collectives: 34.2 us -> 84.8 us
  between operations: 13.6 us -> 0.22 us
  starting transfers between devices: 22.2 us -> 34.1 us
    ppermute x0 -> x3, waiting for transfers between devices: none -> 135 us  [close_the_keys(): b_now = lax.ppermute(all_rows, row_axis, perm=q)]
    psum x1, blocking collectives: 34.2 us -> 84.8 us  [body(): lax.psum(partial_value.reshape(owners_count * capacity, adapters_here * r...]
    ppermute x0 -> x3, starting transfers between devices: none -> 11.6 us  [close_the_keys(): b_now = lax.ppermute(all_rows, row_axis, perm=q)]
    psum x1 -> x0, waiting for transfers between devices: 9.39 us -> none  [body(): full = lax.psum(partial_value, 'mp')]
  transfers between devices with their start and end apart: 4 -> 6, of which waited for: 4 -> 5; matrix products, arithmetic and copies ran while one was open for 3% -> 1% of each run, Pallas kernels for 0% -> 0%
where the time goes in v1:
time: 298 us; the launch traced here: 293 us
  waiting for transfers between devices  151 us (51%)
  blocking collectives  84.8 us (28%)
  starting transfers between devices  34.1 us (11%)
  matrix products  18.2 us (6%)
  other arithmetic  3.59 us (1%)
    ppermute x3, waiting for transfers between devices, close_the_keys(): b_now = lax.ppermute(all_rows, row_axis, perm=q)  135 us
    psum x1, blocking collectives, body(): lax.psum(partial_value.reshape(owners_count * capacity, adapters_here * r...  84.8 us
    ppermute x3, starting transfers between devices, close_the_keys(): b_now = lax.ppermute(all_rows, row_axis, perm=q)  11.6 us
    all_to_all x1, waiting for transfers between devices, body(): lax.all_to_all(send_rows, 'dp', split_axis=0, concat_axis=0, tiled=True)  7.91 us
    all_to_all x1, starting transfers between devices, body(): lax.all_to_all(send_rows, 'dp', split_axis=0, concat_axis=0, tiled=True)  7.62 us
    all_to_all x1, starting transfers between devices, body(): lax.all_to_all(send_ids, 'dp', split_axis=0, concat_axis=0, tiled=True)  7.4 us
    all_to_all x1, starting transfers between devices, body(): back = lax.all_to_all(delta, 'dp', split_axis=0, concat_axis=0, tiled=True)  7.4 us
  transfers between devices with their start and end apart: 6, of which 5 were waited for; matrix products, arithmetic and copies ran while one was open for 1% of the time, Pallas kernels for 0%

profile of v1, /device:TPU:22, one launch (start us, length us, event | category | flops | bytes accessed | tf_op | source)
XLA Modules:
  0.0 292.9 jit_solution(11947067583230288643)
XLA Ops:
  0.0 0.0 copy-start
  0.0 0.8 iota_compare_fusion.6
  0.8 1.2 fusion.40
  2.1 0.8 bitcast_convert_fusion
  2.9 4.6 %fusion.46 = (f32[128,8]{1,0:T(8,128)S(1)}, f32[128,8,128]{2,1,0:T(8,128)S(1)}) fusion(bf16[128,8,128]{2,1,0:T(8,128)(2,1)} %param.12, bf16[128,1,128,128]{3,2,1,0:T(8,128)(2,1)} %param.13, pred[128,128]{1,0:T(8,128)(4,1)S(1)} %iota_compare_fusion.6), kind=kOutput, calls=%fused_computation.62 | convolution fusion | flops 33946624 | bytes 5001216 | tf_op jit(solution)/shard_map/bgjd,bgtd->bgjt/dot_general | solution.py:15
  7.5 0.1 copy.19
  7.6 0.1 copy.20
  7.7 0.4 fusion.22
  8.1 0.1 copy.22
  8.3 0.1 copy.23
  8.4 3.5 %fusion.16 = bf16[128,8,128]{2,1,0:T(8,128)(2,1)S(1)} fusion(bf16[128,1,128,128]{3,2,1,0:T(8,128)(2,1)} %param.14, f32[128,8,128]{2,1,0:T(8,128)S(1)} %get-tuple-element.10, f32[128,128]{1,0:T(8,128)S(1)} %bitcast_convert_fusion, f32[128,8]{1,0:T(8,128)S(1)} %copy.23, f32[128,8]{1,0:T(8,128)S(1)} %copy.22, f32[128,8]{1,0:T(8,128)S(1)} %copy.20), kind=kOutput, calls=%fused_computation.14 | convolution fusion | flops 34340864 | bytes 5058560 | tf_op jit(solution)/shard_map/bgjt,bgtd->bgjd/dot_general | solution.py:29
  11.8 4.6 %fusion.24 = f32[128,4096]{1,0:T(8,128)S(1)} fusion(bf16[1024,4096]{1,0:T(8,128)(2,1)} %param.21, bf16[16,8,8,128]{3,2,1,0:T(8,128)(2,1)S(1)} %bitcast.77), kind=kOutput, calls=%fused_computation.22 | convolution fusion | flops 1073741824 | bytes 10747904 | tf_op jit(solution)/shard_map/dot_general | solution.py:83
  16.5 0.0 copy-start.2
  16.5 0.0 copy-start.3
  16.5 2.0 collective-permute-start
  18.5 45.6 %collective-permute-done = f32[128,4096]{1,0:T(8,128)S(1)} collective-permute-done((f32[128,4096]{1,0:T(8,128)S(1)}, f32[128,4096]{1,0:T(8,128)S(1)}, u32[]{:S(2)}, u32[]{:S(2)}) %collective-permute-start) | collective-permute-done | bytes 2097184 | tf_op jit(solution)/shard_map/ppermute | solution.py:89
  64.1 0.3 add.74
  64.5 3.4 %collective-permute-start.1 = (f32[128,4096]{1,0:T(8,128)S(1)}, f32[128,4096]{1,0:T(8,128)S(1)}, u32[]{:S(2)}, u32[]{:S(2)}) collective-permute-start(f32[128,4096]{1,0:T(8,128)S(1)} %add.74), channel_id=1, source_target_pairs={{0,2},{1,3},{2,0},{3,1},{4,6},{5,7},{6,4},{7,5},{8,10},{9,11},{10,... | collective-permute-start | bytes 6291464 | tf_op jit(solution)/shard_map/ppermute | solution.py:89
  67.8 0.0 copy-done.2
  67.8 0.0 copy-done.3
  67.8 0.4 select_reduce_fusion
  68.3 89.5 %collective-permute-done.1 = f32[128,4096]{1,0:T(8,128)S(1)} collective-permute-done((f32[128,4096]{1,0:T(8,128)S(1)}, f32[128,4096]{1,0:T(8,128)S(1)}, u32[]{:S(2)}, u32[]{:S(2)}) %collective-permute-start.1) | collective-permute-done | bytes 2097184 | tf_op jit(solution)/shard_map/ppermute | solution.py:89
  157.7 0.2 add.75
  158.0 0.0 copy-start.1
  158.0 6.3 %collective-permute-start.2 = (f32[128,4096]{1,0:T(8,128)S(1)}, f32[128,4096]{1,0:T(8,128)}, u32[]{:S(2)}, u32[]{:S(2)}) collective-permute-start(f32[128,4096]{1,0:T(8,128)S(1)} %add.75), channel_id=1, source_target_pairs={{0,4},{1,5},{2,6},{3,7},{4,0},{5,1},{6,2},{7,3},{8,12},{9,13},{10,... | collective-permute-start | bytes 6291464 | tf_op jit(solution)/shard_map/ppermute | solution.py:89
  164.2 0.1 fusion.39
  164.3 0.2 reduce_window_sum.11
  164.5 0.2 select_reduce_fusion.2
  164.7 0.1 select_reduce_fusion.1
  164.8 0.7 all_to_all.12
  165.5 7.4 %all-to-all-start = ((s32[32,1,8]{2,1,0:T(1,128)}), s32[32,1,8]{2,1,0:T(1,128)S(1)}, u32[]{:S(2)}, u32[]{:S(2)}) async-start(s32[32,1,8]{2,1,0:T(1,128)} %bitcast.6), calls=%async_computation | async-start | bytes 32768 | tf_op jit(solution)/shard_map/all_to_all | solution.py:96
  172.9 0.0 copy-start.4
  172.9 1.1 fusion.4
  174.0 2.5 all-to-all-done
  176.5 7.6 %all-to-all-start.1 = ((bf16[32,8,1024]{2,1,0:T(8,128)(2,1)}), bf16[32,8,1024]{2,1,0:T(8,128)(2,1)S(1)}, u32[]{:S(2)}, u32[]{:S(2)}) async-start(bf16[32,8,1024]{2,1,0:T(8,128)(2,1)} %fusion.4), calls=%async_computation.1 | async-start | bytes 1048576 | tf_op jit(solution)/shard_map/all_to_all | solution.py:95
  184.2 0.1 sub.34
  184.3 7.9 %all-to-all-done.1 = bf16[32,8,1024]{2,1,0:T(8,128)(2,1)S(1)} async-done(((bf16[32,8,1024]{2,1,0:T(8,128)(2,1)}), bf16[32,8,1024]{2,1,0:T(8,128)(2,1)S(1)}, u32[]{:S(2)}, u32[]{:S(2)}) %all-to-all-start.1) | async-done | bytes 524320 | tf_op jit(solution)/shard_map/all_to_all | solution.py:95
  192.2 0.0 copy-done
  192.2 0.3 fusion.20
  192.5 84.8 %all-reduce.1 = bf16[256,128]{0,1:T(8,128)(2,1)S(1)} all-reduce(f32[256,128]{0,1:T(8,128)S(1)} %bitcast.80), channel_id=1, replica_groups=mesh['dp'=32,'mp'=8] {'mp'}, use_global_device_ids=true, to_apply=%region_6.7 | all-reduce | flops 32768 | bytes 196608 | tf_op jit(solution)/shard_map/psum | solution.py:104
  277.3 0.0 copy-done.1
  277.3 1.0 fusion.19
  278.3 7.4 %all-to-all-start.2 = ((bf16[32,8,512]{2,1,0:T(8,128)(2,1)}), bf16[32,8,512]{2,1,0:T(8,128)(2,1)S(1)}, u32[]{:S(2)}, u32[]{:S(2)}) async-start(bf16[32,8,512]{2,1,0:T(8,128)(2,1)} %fusion.19), calls=%async_computation.2 | async-start | bytes 524288 | tf_op jit(solution)/shard_map/all_to_all | solution.py:110
  285.7 0.0 copy-done.4
  285.7 5.3 %all-to-all-done.2 = bf16[32,8,512]{2,1,0:T(8,128)(2,1)S(1)} async-done(((bf16[32,8,512]{2,1,0:T(8,128)(2,1)}), bf16[32,8,512]{2,1,0:T(8,128)(2,1)S(1)}, u32[]{:S(2)}, u32[]{:S(2)}) %all-to-all-start.2) | async-done | bytes 262176 | tf_op jit(solution)/shard_map/all_to_all | solution.py:110
  291.0 0.0 collective-permute-done.2
  291.0 1.8 fusion.28
  (10 shorter events, 0.2 us)
Async XLA Ops:
  0.0 192.2 %copy-start = (bf16[2,1024,64]{1,2,0:T(8,128)(2,1)S(1)}, bf16[2,1024,64]{1,2,0:T(8,128)(2,1)}, u32[]{:S(2)}) copy-start(bf16[2,1024,64]{1,2,0:T(8,128)(2,1)} %param.22) | copy-start | bytes 786436
  16.5 51.3 %copy-start.2 = (s32[4096]{0:T(1024)S(1)}, s32[4096]{0:T(1024)}, u32[]{:S(2)}) copy-start(s32[4096]{0:T(1024)} %param.20) | copy-start | bytes 49156
  16.5 51.3 %copy-start.3 = (s32[128]{0:T(128)S(1)}, s32[128]{0:T(128)}, u32[]{:S(2)}) copy-start(s32[128]{0:T(128)} %param.19) | copy-start | bytes 1540
  16.5 47.6 %collective-permute-start = (f32[128,4096]{1,0:T(8,128)S(1)}, f32[128,4096]{1,0:T(8,128)S(1)}, u32[]{:S(2)}, u32[]{:S(2)}) collective-permute-start(f32[128,4096]{1,0:T(8,128)S(1)} %fusion.24), channel_id=1, source_target_pairs={{0,1},{1,0},{2,3},{3,2},{4,5},{5,4},{6,7},{7,6},{8,9},{9,8},{10,11... | collective-permute-start | bytes 6291464 | tf_op jit(solution)/shard_map/ppermute | solution.py:89
  64.5 93.3 %collective-permute-start.1 = (f32[128,4096]{1,0:T(8,128)S(1)}, f32[128,4096]{1,0:T(8,128)S(1)}, u32[]{:S(2)}, u32[]{:S(2)}) collective-permute-start(f32[128,4096]{1,0:T(8,128)S(1)} %add.74), channel_id=1, source_target_pairs={{0,2},{1,3},{2,0},{3,1},{4,6},{5,7},{6,4},{7,5},{8,10},{9,11},{10,... | collective-permute-start | bytes 6291464 | tf_op jit(solution)/shard_map/ppermute | solution.py:89
  158.0 119.4 %copy-start.1 = (bf16[2,64,512]{2,1,0:T(8,128)(2,1)S(1)}, bf16[2,64,512]{2,1,0:T(8,128)(2,1)}, u32[]{:S(2)}) copy-start(bf16[2,64,512]{2,1,0:T(8,128)(2,1)} %param.23) | copy-start | bytes 393220
  158.0 133.0 %collective-permute-start.2 = (f32[128,4096]{1,0:T(8,128)S(1)}, f32[128,4096]{1,0:T(8,128)}, u32[]{:S(2)}, u32[]{:S(2)}) collective-permute-start(f32[128,4096]{1,0:T(8,128)S(1)} %add.75), channel_id=1, source_target_pairs={{0,4},{1,5},{2,6},{3,7},{4,0},{5,1},{6,2},{7,3},{8,12},{9,13},{10,... | collective-permute-start | bytes 6291464 | tf_op jit(solution)/shard_map/ppermute | solution.py:89
  165.5 11.0 %all-to-all-start = ((s32[32,1,8]{2,1,0:T(1,128)}), s32[32,1,8]{2,1,0:T(1,128)S(1)}, u32[]{:S(2)}, u32[]{:S(2)}) async-start(s32[32,1,8]{2,1,0:T(1,128)} %bitcast.6), calls=%async_computation | async-start | bytes 32768 | tf_op jit(solution)/shard_map/all_to_all | solution.py:96
  172.9 112.8 %copy-start.4 = (s32[128]{0:T(128)S(1)}, s32[128]{0:T(128)}, u32[]{:S(2)}) copy-start(s32[128]{0:T(128)} %param.18) | copy-start | bytes 1540
  176.5 15.7 %all-to-all-start.1 = ((bf16[32,8,1024]{2,1,0:T(8,128)(2,1)}), bf16[32,8,1024]{2,1,0:T(8,128)(2,1)S(1)}, u32[]{:S(2)}, u32[]{:S(2)}) async-start(bf16[32,8,1024]{2,1,0:T(8,128)(2,1)} %fusion.4), calls=%async_computation.1 | async-start | bytes 1048576 | tf_op jit(solution)/shard_map/all_to_all | solution.py:95
  278.3 12.7 %all-to-all-start.2 = ((bf16[32,8,512]{2,1,0:T(8,128)(2,1)}), bf16[32,8,512]{2,1,0:T(8,128)(2,1)S(1)}, u32[]{:S(2)}, u32[]{:S(2)}) async-start(bf16[32,8,512]{2,1,0:T(8,128)(2,1)} %fusion.19), calls=%async_computation.2 | async-start | bytes 524288 | tf_op jit(solution)/shard_map/all_to_all | solution.py:110
